TPU v7x, 512 devices: a whole 4x8x8 slice. The times are simulated.
512 devices in a mesh: rep: 8 (over z_hi, core), fsdp: 64 (over y, x, z_lo).
Axes of the slice: x: 4, y: 8, z: 8 (z_hi: 4, z_lo: 2; z = z_hi * 2 + z_lo), core: 2. Of those that a mesh axis runs over, the one named last changes fastest.
Arguments:
- acts: bfloat16 [8, 8192, 8192], P('rep', 'fsdp'), may hold values from -16 to 16
- value_cots: bfloat16 [8, 8192, 512], P('rep', 'fsdp'), may hold values from -0.059814453 to 0.059814453
- inner_weights: float32 [8, 8192, 512], P('rep', 'fsdp'), may hold values from -0.0625 to 0.0625
- first_moment: float32 [8, 8192, 512], P('rep', 'fsdp'), may hold values from -1.8 to 1.8
- second_moment: float32 [8, 8192, 512], P('rep', 'fsdp'), may hold values from 0.01 to 1
- anchor: float32 [8192, 512], P('fsdp'), may hold values from -0.0625 to 0.0625
- outer_momentum: float32 [8192, 512], P('fsdp'), may hold values from -0.06 to 0.06
Outputs:
- first_next: float32 [8, 8192, 512], P('rep', 'fsdp')
- values_next: bfloat16 [8, 8192, 512], P('rep', 'fsdp')
All inputs are finite; a program needn't handle non-finite values.
Results may differ from a plain program's by a relative error of at most 0.0049.
Values may be sent and summed in bfloat16 or wider, within the bound.
A program may use at most 64 MiB of HBM per device.

v0:
```python
import jax
import jax.numpy as jnp
from jax import lax
from jax.sharding import PartitionSpec as P

decay_first = 0.9
decay_second = 0.95
inner_rate = 0.006
epsilon = 1e-08
outer_rate = 0.7
outer_decay = 0.9


def outer_update(average, anchor_rows, momentum_rows):
    velocity = outer_decay * momentum_rows + average
    return (anchor_rows - outer_rate * (average + outer_decay * velocity)).astype(jnp.bfloat16)


def on_device(acts, value_cots, inner_weights, first_moment, second_moment, anchor, outer_momentum):
    tokens_local = acts[0]
    cots_local = value_cots[0]
    rep_count = lax.axis_size("rep")
    feature_split = lax.all_to_all(tokens_local, "fsdp", split_axis=1, concat_axis=0, tiled=True)
    columns = feature_split
    gradient = lax.dot_general(
        columns,
        lax.all_gather(cots_local, "fsdp", axis=0, tiled=True),
        (((0,), (0,)), ((), ())),
        preferred_element_type=jnp.float32,
    )
    first_next = decay_first * first_moment[0] + (1.0 - decay_first) * gradient
    second_next = decay_second * second_moment[0] + (1.0 - decay_second) * gradient * gradient
    stepped = inner_weights[0] - inner_rate * first_next / (jnp.sqrt(second_next) + epsilon)
    drift = anchor - stepped
    summed_drift = lax.psum(drift, "rep")
    weights_next = outer_update(summed_drift / rep_count, anchor, outer_momentum)
    columns = tokens_local
    values = jnp.dot(
        columns,
        lax.all_gather(weights_next, "fsdp", axis=0, tiled=True),
        preferred_element_type=jnp.float32,
    )
    return (first_next[None], values.astype(jnp.bfloat16)[None])


def solution(mesh):
    placed = (
        P("rep", "fsdp", None),
        P("rep", "fsdp", None),
        P("rep", "fsdp", None),
        P("rep", "fsdp", None),
        P("rep", "fsdp", None),
        P("fsdp", None),
        P("fsdp", None),
    )
    return jax.shard_map(
        on_device,
        mesh=mesh,
        in_specs=placed,
        out_specs=(P("rep", "fsdp", None), P("rep", "fsdp", None)),
        check_vma=False,
    )
```

profile of v0, /device:TPU:2, one launch (start us, length us, event | category | flops | bytes accessed | tf_op | source)
XLA Modules:
  0.0 755.7 jit_solution(2856607011129081235)
XLA Ops:
  7.2 0.0 all-gather.6.cloned.1.call-start
  7.2 0.7 all-gather.6.cloned.1.call-update
  7.9 0.0 all-reduce.2.cloned.1.call-start
  7.9 3.2 copy.11
  11.2 74.7 %all_to_all.19 = bf16[128,64,128]{0,2,1:T(8,128)(2,1)} all-to-all(bf16[128,64,128]{0,2,1:T(8,128)(2,1)S(1)} %bitcast.35), channel_id=1, replica_groups=mesh['rep'=8,'fsdp'=64] {'fsdp'}, dimensions={1} | all-to-all | bytes 4194304 | tf_op jit(solution)/shard_map/all_to_all | solution.py:23
  85.9 0.0 copy-start
  85.9 0.0 copy-start.1
  85.9 0.0 copy-start.2
  85.9 0.0 copy-start.3
  85.9 3.3 copy.12
  89.2 248.0 %all-gather.6.cloned.1.call-done = bf16[1,8192,512]{2,1,0:T(8,128)(2,1)} async-done(((bf16[1,128,512]{2,1,0:T(8,128)(2,1)}), bf16[1,8192,512]{2,1,0:T(8,128)(2,1)}) %all-gather.6.cloned.1.call-update) | async-done | bytes 8388624 | tf_op jit(solution)/shard_map/all_gather | solution.py:27
  337.2 0.0 copy-done
  337.2 0.0 copy-done.1
  337.2 0.0 copy-done.2
  337.2 0.0 copy-done.3
  337.2 0.0 copy-start.4
  337.2 5.7 fusion.15
  342.9 0.0 all-reduce.2.cloned.1.call-update
  342.9 0.0 all-gather.4.cloned.1.call-start
  343.0 82.9 %all-reduce.2.cloned.1.call-done = f32[128,512]{1,0:T(8,128)} async-done(((f32[128,512]{1,0:T(8,128)}), f32[128,512]{1,0:T(8,128)}) %all-reduce.2.cloned.1.call-update) | async-done | bytes 262160 | tf_op jit(solution)/shard_map/psum | solution.py:35
  425.8 0.0 copy-done.4
  425.8 1.7 subtract_convert_fusion
  427.5 0.0 all-gather.4.cloned.1.call-update
  427.6 314.5 %all-gather.4.cloned.1.call-done = bf16[8192,512]{1,0:T(8,128)(2,1)} async-done(((bf16[128,512]{1,0:T(8,128)(2,1)}), bf16[8192,512]{1,0:T(8,128)(2,1)}) %all-gather.4.cloned.1.call-update) | async-done | bytes 8388624 | tf_op jit(solution)/shard_map/all_gather | solution.py:40
  742.1 6.4 fusion.7
  748.4 0.8 copy.13
Async XLA Ops:
  7.2 330.1 %all-gather.6.cloned.1.call-start = ((), (), s32[]{:S(2)}) async-start(), calls=%async_computation.3 | async-start | bytes 8519680 | tf_op jit(solution)/shard_map/all_gather | solution.py:27
  7.9 417.9 %all-reduce.2.cloned.1.call-start = ((), (), s32[]{:S(2)}) async-start(), calls=%async_computation.1 | async-start | bytes 524288 | tf_op jit(solution)/shard_map/psum | solution.py:35
  85.9 251.4 %copy-start = (f32[128,512]{1,0:T(8,128)S(1)}, f32[128,512]{1,0:T(8,128)}, u32[]{:S(2)}) copy-start(f32[128,512]{1,0:T(8,128)} %param.12) | copy-start | bytes 786436
  85.9 251.4 %copy-start.1 = (f32[1,128,512]{2,1,0:T(8,128)S(1)}, f32[1,128,512]{2,1,0:T(8,128)}, u32[]{:S(2)}) copy-start(f32[1,128,512]{2,1,0:T(8,128)} %param.9) | copy-start | bytes 786436
  85.9 251.4 %copy-start.2 = (f32[1,128,512]{2,1,0:T(8,128)S(1)}, f32[1,128,512]{2,1,0:T(8,128)}, u32[]{:S(2)}) copy-start(f32[1,128,512]{2,1,0:T(8,128)} %param.11) | copy-start | bytes 786436
  85.9 251.4 %copy-start.3 = (f32[1,128,512]{2,1,0:T(8,128)S(1)}, f32[1,128,512]{2,1,0:T(8,128)}, u32[]{:S(2)}) copy-start(f32[1,128,512]{2,1,0:T(8,128)} %param.10) | copy-start | bytes 786436
  337.2 88.6 %copy-start.4 = (f32[128,512]{1,0:T(8,128)S(1)}, f32[128,512]{1,0:T(8,128)}, u32[]{:S(2)}) copy-start(f32[128,512]{1,0:T(8,128)} %param.13) | copy-start | bytes 786436
  342.9 399.1 %all-gather.4.cloned.1.call-start = ((), (), s32[]{:S(2)}) async-start(), calls=%async_computation.2 | async-start | bytes 8519680 | tf_op jit(solution)/shard_map/all_gather | solution.py:40
Sparse Core Ops, SparseCore 0:
  10.1 327.0 all-gather.5
  343.1 82.7 all-reduce.1
  428.7 313.3 all-gather.3
where the time goes:
time: 756 us
  waiting for transfers between devices  646 us (85%)
  blocking collectives  74.7 us (10%)
  between operations  13.8 us (2%)
  matrix products  12 us (2%)
    all_gather x1, waiting for transfers between devices, on_device(): lax.all_gather(weights_next, 'fsdp', axis=0, tiled=True)  315 us
    all_gather x1, waiting for transfers between devices, on_device(): lax.all_gather(cots_local, 'fsdp', axis=0, tiled=True)  248 us
    psum x1, waiting for transfers between devices, on_device(): summed_drift = lax.psum(drift, 'rep')  82.9 us
    all_to_all x1, blocking collectives, on_device(): lax.all_to_all(tokens_local, 'fsdp', split_axis=1, concat_axis=0, tiled=T...  74.7 us
  transfers between devices with their start and end apart: 3, of which 3 were waited for; matrix products, arithmetic and copies ran while one was open for 1% of the time, Pallas kernels for 0%

commit v1 on v0

v1 whole, which is shorter than its diff:
```python
import jax
import jax.numpy as jnp
from jax import lax
from jax.experimental import pallas as pl
from jax.experimental.pallas import tpu as pltpu
from jax.sharding import PartitionSpec as P

decay_first = 0.9
decay_second = 0.95
inner_rate = 0.006
epsilon = 1e-08
outer_rate = 0.7
outer_decay = 0.9

MESH = pl.DeviceIdType.MESH
F32 = jnp.float32
BF16 = jnp.bfloat16

Y = 8
J = 8
Z = 4
B = 128
C = 512
OFFSETS = (4, 3, 5, 2, 6, 1, 7, 0)
SLOT = {off: k for k, off in enumerate(OFFSETS)}
OWN = SLOT[0]


def step_kernel(
    acts, cots, inner, first, second, anchor, momentum, first_out, values_out,
    a_buf, c_buf, state, first_buf, go_up, go_down, from_down, from_up,
    drift_buf, drift_pair, pair_sum, z_buf, w_buf, v_send, v_recv,
    state_sem, cots_s, cots_r, acts_s, acts_r, up_s, up_r, down_s, down_r,
    pair_s, pair_r, z_s, z_r, wz_s, wz_r, wy_s, wy_r, wc_s, wc_r, v_s, v_r, out_sem,
):
    f = lax.axis_index("fsdp")
    r = lax.axis_index("rep")
    y, j = lax.div(f, J), lax.rem(f, J)
    zh, core = lax.div(r, 2), lax.rem(r, 2)

    def in_plane(d):
        return {"fsdp": y * J + lax.rem(j + d, J)}

    def along_y(t):
        return {"fsdp": lax.rem(y + t, Y) * J + j}

    def along_z(q):
        return {"rep": lax.rem(zh + q, Z) * 2 + core}

    sibling = {"rep": zh * 2 + 1 - core}

    def remote(src, dst, send, recv, device):
        return pltpu.make_async_remote_copy(
            src_ref=src, dst_ref=dst, send_sem=send, recv_sem=recv, device_id=device, device_id_type=MESH
        )

    def rows(start, size):
        return pl.ds(pl.multiple_of(start, size), size)

    loads = [
        pltpu.make_async_copy(ref, state.at[i], state_sem.at[i])
        for i, ref in enumerate((inner, first, second, anchor, momentum))
    ]
    for load in loads:
        load.start()
    own_cots = pltpu.make_async_copy(cots, c_buf.at[rows(j * B, B)], cots_r.at[0])
    own_cots.start()

    def acts_block(k, target):
        return acts.at[:, rows((lax.rem(y + OFFSETS[k], Y) * J + target) * B, B)]

    own_acts = []
    for k in range(Y):
        copy = pltpu.make_async_copy(
            acts_block(k, j), a_buf.at[rows(j * B, B), pl.ds(k * B, B)], acts_r.at[k, 0]
        )
        copy.start()
        own_acts.append(copy)

    barrier = pltpu.get_barrier_semaphore()
    for d in range(1, J):
        pl.semaphore_signal(barrier, inc=1, device_id=in_plane(d), device_id_type=MESH)
    for t in range(1, Y):
        pl.semaphore_signal(barrier, inc=1, device_id=along_y(t), device_id_type=MESH)
    for q in range(1, Z):
        pl.semaphore_signal(barrier, inc=1, device_id=along_z(q), device_id_type=MESH)
    pl.semaphore_signal(barrier, inc=1, device_id=sibling, device_id_type=MESH)
    pl.semaphore_wait(barrier, J - 1 + Y - 1 + Z - 1 + 1)

    def cots_copy(d):
        return remote(cots, c_buf.at[rows(j * B, B)], cots_s.at[d], cots_r.at[d], in_plane(d))

    def cots_arrival(d):
        return remote(cots, c_buf.at[rows(lax.rem(j + J - d, J) * B, B)], cots_s.at[d], cots_r.at[d], in_plane(d))

    def acts_copy(k, d):
        return remote(
            acts_block(k, lax.rem(j + d, J)), a_buf.at[rows(j * B, B), pl.ds(k * B, B)],
            acts_s.at[k, d], acts_r.at[k, d], in_plane(d),
        )

    def acts_arrival(k, d):
        return remote(
            acts_block(k, j), a_buf.at[rows(lax.rem(j + J - d, J) * B, B), pl.ds(k * B, B)],
            acts_s.at[k, d], acts_r.at[k, d], in_plane(d),
        )

    def each(low, high, body):
        def step(i, carry):
            body(i)
            return carry

        lax.fori_loop(low, high, step, 0)

    each(1, J, lambda d: cots_copy(d).start())
    for k in range(Y):
        each(1, J, lambda d, k=k: acts_copy(k, d).start())

    own_cots.wait()
    each(1, J, lambda d: cots_arrival(d).wait_recv())

    def partial_gradient(k):
        own_acts[k].wait()
        each(1, J, lambda d: acts_arrival(k, d).wait_recv())
        return lax.dot_general(
            a_buf[:, pl.ds(k * B, B)], c_buf[...], (((0,), (0,)), ((), ())), preferred_element_type=F32
        )

    half = C // 2
    low, high = pl.ds(0, half), pl.ds(half, half)
    part = partial_gradient(SLOT[4])
    go_up[0, :, low] = part[:, :half]
    go_down[0, :, high] = part[:, half:]

    def up_copy(i):
        cols = low if i == 0 else pl.ds(0, C)
        return remote(go_up.at[i, :, cols], from_down.at[i, :, cols], up_s.at[i], up_r.at[i], along_y(1))

    def down_copy(i):
        cols = high if i == 0 else pl.ds(0, C)
        return remote(go_down.at[i, :, cols], from_up.at[i, :, cols], down_s.at[i], down_r.at[i], along_y(Y - 1))

    ups = [up_copy(i) for i in range(4)]
    downs = [down_copy(i) for i in range(4)]
    ups[0].start()
    downs[0].start()
    for i in range(1, 4):
        part = partial_gradient(SLOT[4 - i])
        ups[i - 1].wait_recv()
        if i == 1:
            go_up[1, :, low] = part[:, :half] + from_down[0, :, low]
            go_up[1, :, high] = part[:, half:]
        else:
            go_up[i] = part + from_down[i - 1]
        ups[i].start()
        part = partial_gradient(SLOT[4 + i])
        downs[i - 1].wait_recv()
        if i == 1:
            go_down[1, :, low] = part[:, :half]
            go_down[1, :, high] = part[:, half:] + from_up[0, :, high]
        else:
            go_down[i] = part + from_up[i - 1]
        downs[i].start()
    part = partial_gradient(OWN)
    ups[3].wait_recv()
    downs[3].wait_recv()
    gradient = part + from_down[3] + from_up[3]

    for load in loads:
        load.wait()
    first_next = decay_first * state[1] + (1.0 - decay_first) * gradient
    first_buf[...] = first_next
    store_first = pltpu.make_async_copy(first_buf, first_out, out_sem)
    store_first.start()
    second_next = decay_second * state[2] + (1.0 - decay_second) * gradient * gradient
    stepped = state[0] - inner_rate * first_next / (jnp.sqrt(second_next) + epsilon)
    drift_buf[...] = state[3] - stepped

    H = B // 2
    Q = H // Z
    pair = remote(drift_buf.at[rows((1 - core) * H, H)], drift_pair, pair_s, pair_r, sibling)
    pair.start()
    pair.wait_recv()
    pair_sum[...] = drift_buf[rows(core * H, H), :] + drift_pair[...]

    def z_copy(q):
        return remote(
            pair_sum.at[rows(lax.rem(zh + q, Z) * Q, Q)], z_buf.at[q], z_s.at[q], z_r.at[q], along_z(q)
        )

    zs = [z_copy(q) for q in range(1, Z)]
    for copy in zs:
        copy.start()
    total = pair_sum[rows(zh * Q, Q), :]
    for q in range(1, Z):
        zs[q - 1].wait_recv()
        total = total + z_buf[q]
    mine = core * H + zh * Q
    anchor_rows = state[3, rows(mine, Q), :]
    momentum_rows = state[4, rows(mine, Q), :]
    average = total / (2 * Z)
    velocity = outer_decay * momentum_rows + average
    weights = (anchor_rows - outer_rate * (average + outer_decay * velocity)).astype(BF16)
    w_buf[rows(OWN * B + mine, Q), :] = weights

    def wz_copy(q):
        here = w_buf.at[rows(OWN * B + mine, Q)]
        return remote(here, here, wz_s.at[q], wz_r.at[q], along_z(q))

    def wz_arrival(q):
        there = w_buf.at[rows(OWN * B + core * H + lax.rem(zh + Z - q, Z) * Q, Q)]
        return remote(there, there, wz_s.at[q], wz_r.at[q], along_z(q))

    wzs = [wz_copy(q) for q in range(1, Z)]
    for copy in wzs:
        copy.start()
    for q in range(1, Z):
        wz_arrival(q).wait_recv()

    def w_half(t, side):
        return w_buf.at[rows(SLOT[(Y - t) % Y] * B + side * H, H)]

    near_first = (4, 3, 5, 2, 6, 1, 7)
    wys = {t: remote(w_half(0, core), w_half(t, core), wy_s.at[t], wy_r.at[t], along_y(t)) for t in near_first}
    for t in near_first:
        wys[t].start()
    forwards = {t: remote(w_half(t, core), w_half(t, core), wc_s.at[t], wc_r.at[t], sibling) for t in range(Y)}
    forwards[0].start()
    for t in reversed(near_first):
        wys[t].wait_recv()
        forwards[t].start()
    for t in range(Y):
        remote(w_half(t, 1 - core), w_half(t, 1 - core), wc_s.at[t], wc_r.at[t], sibling).wait_recv()

    def values_of(target):
        return jnp.dot(a_buf[rows(target * B, B), :], w_buf[...], preferred_element_type=F32)

    def v_copy(d):
        return remote(v_send.at[d], v_recv.at[d], v_s.at[d], v_r.at[d], in_plane(d))

    def send_values(d):
        v_send[d] = values_of(lax.rem(j + d, J)).astype(BF16)
        v_copy(d).start()

    each(1, J, send_values)
    total = values_of(j)
    for d in range(1, J):
        v_copy(d).wait_recv()
        total = total + v_recv[d].astype(F32)
    values_out[...] = total.astype(BF16)

    store_first.wait()
    each(1, J, lambda d: cots_copy(d).wait_send())
    for k in range(Y):
        each(1, J, lambda d, k=k: acts_copy(k, d).wait_send())
    for i in range(4):
        ups[i].wait_send()
        downs[i].wait_send()
    pair.wait_send()
    for copy in zs + wzs:
        copy.wait_send()
    for t in near_first:
        wys[t].wait_send()
    for t in range(Y):
        forwards[t].wait_send()
    each(1, J, lambda d: v_copy(d).wait_send())


def on_device(acts, value_cots, inner_weights, first_moment, second_moment, anchor, outer_momentum):
    dma = pltpu.SemaphoreType.DMA
    vmem = pltpu.VMEM
    first_next, values = pl.pallas_call(
        step_kernel,
        name="diloco_step",
        out_shape=(jax.ShapeDtypeStruct((B, C), F32), jax.ShapeDtypeStruct((B, C), BF16)),
        in_specs=[pl.BlockSpec(memory_space=pl.ANY)] * 7,
        out_specs=(pl.BlockSpec(memory_space=pl.ANY), pl.BlockSpec(memory_space=pltpu.VMEM)),
        scratch_shapes=[
            vmem((J * B, Y * B), BF16),
            vmem((J * B, C), BF16),
            vmem((5, B, C), F32),
            vmem((B, C), F32),
            vmem((4, B, C), F32),
            vmem((4, B, C), F32),
            vmem((4, B, C), F32),
            vmem((4, B, C), F32),
            vmem((B, C), F32),
            vmem((B // 2, C), F32),
            vmem((B // 2, C), F32),
            vmem((Z, B // 2 // Z, C), F32),
            vmem((Y * B, C), BF16),
            vmem((J, B, C), BF16),
            vmem((J, B, C), BF16),
            dma((5,)),
            dma((J,)), dma((J,)),
            dma((Y, J)), dma((Y, J)),
            dma((4,)), dma((4,)), dma((4,)), dma((4,)),
            dma(()), dma(()),
            dma((Z,)), dma((Z,)),
            dma((Z,)), dma((Z,)),
            dma((Y,)), dma((Y,)),
            dma((Y,)), dma((Y,)),
            dma((J,)), dma((J,)),
            dma(()),
        ],
        compiler_params=pltpu.CompilerParams(
            collective_id=0, has_side_effects=True, vmem_limit_bytes=40 * 1024 * 1024
        ),
    )(acts[0], value_cots[0], inner_weights[0], first_moment[0], second_moment[0], anchor, outer_momentum)
    return first_next[None], values[None]


def solution(mesh):
    placed = (
        P("rep", "fsdp", None),
        P("rep", "fsdp", None),
        P("rep", "fsdp", None),
        P("rep", "fsdp", None),
        P("rep", "fsdp", None),
        P("fsdp", None),
        P("fsdp", None),
    )
    return jax.shard_map(
        on_device,
        mesh=mesh,
        in_specs=placed,
        out_specs=(P("rep", "fsdp", None), P("rep", "fsdp", None)),
        check_vma=False,
    )
```

time: 756 us -> 115 us (0.15)
  the two profiles are of different devices: /device:TPU:2 before, /device:TPU:1 now
where the time goes in v1:
time: 115 us
  Pallas kernels  106 us (92%)
  local copies, waits for them, and re-layouts  8.6 us (7%)
    pallas_call x1, Pallas kernels, on_device(): pl.pallas_call(step_kernel, name='diloco_step', out_shape=(jax.ShapeDtype...  106 us
    unnamed x16, local copies, waits for them, and re-layouts  8.6 us

profile of v1, /device:TPU:1, one launch (start us, length us, event | category | flops | bytes accessed | tf_op | source)
XLA Modules:
  0.0 114.8 jit_solution(18251092621223216369)
XLA Ops:
  0.6 0.0 copy-start
  0.6 1.6 %copy-done = bf16[1,128,8192]{2,1,0:T(8,128)(2,1)S(1)} copy-done((bf16[1,128,8192]{2,1,0:T(8,128)(2,1)S(1)}, bf16[1,128,8192]{2,1,0:T(8,128)(2,1)}, u32[]{:S(2)}) %copy-start) | copy-done | bytes 2097176
  2.2 0.0 copy-start.1
  2.2 0.9 copy-done.1
  3.2 0.0 copy-start.2
  3.2 0.9 copy-done.2
  4.1 0.0 copy-start.3
  4.1 0.9 copy-done.3
  5.1 0.0 copy-start.4
  5.1 0.9 copy-done.4
  6.0 0.0 copy-start.5
  6.0 0.9 copy-done.5
  7.0 0.0 copy-start.6
  7.0 0.9 copy-done.6
  7.9 105.6 %diloco_step.1 = (f32[128,512]{1,0:T(8,128)S(1)}, bf16[128,512]{1,0:T(8,128)(2,1)S(1)}) custom-call(bf16[128,8192]{1,0:T(8,128)(2,1)S(1)} %bitcast.7, bf16[128,512]{1,0:T(8,128)(2,1)S(1)} %bitcast.12, f32[128,512]{1,0:T(8,128)S(1)} %bitcast.8, f32[128,512]{1,0:T(8,128)S(1)} %bitcast.9, f32[128,512]{1,0:T(8,128)S(1)} %bitcast.10, f32[128,512]{1,0:T(8,128)S(1)} %copy-done.4, ...), custom_call_target="tpu_custom_call" | custom-call | tf_op jit(solution)/shard_map/diloco_step/pallas_call | solution.py:272
  113.4 0.7 copy.11
  114.2 0.7 copy.12
Async XLA Ops:
  0.6 1.6 %copy-start = (bf16[1,128,8192]{2,1,0:T(8,128)(2,1)S(1)}, bf16[1,128,8192]{2,1,0:T(8,128)(2,1)}, u32[]{:S(2)}) copy-start(bf16[1,128,8192]{2,1,0:T(8,128)(2,1)} %param.7) | copy-start | bytes 6291460
  2.2 0.9 copy-start.1
  3.2 0.9 copy-start.2
  4.1 0.9 copy-start.3
  5.1 0.9 copy-start.4
  6.0 0.9 copy-start.5
  7.0 0.9 copy-start.6

commit v2 on v0

v2 whole, which is shorter than its diff:
```python
import jax
import jax.numpy as jnp
from jax import lax
from jax.experimental import pallas as pl
from jax.experimental.pallas import tpu as pltpu
from jax.sharding import PartitionSpec as P

decay_first = 0.9
decay_second = 0.95
inner_rate = 0.006
epsilon = 1e-08
outer_rate = 0.7
outer_decay = 0.9

MESH = pl.DeviceIdType.MESH
F32 = jnp.float32
BF16 = jnp.bfloat16

Y = 8
J = 8
Z = 4
B = 128
C = 512
OFFSETS = (4, 3, 5, 2, 6, 1, 7, 0)
SLOT = {off: k for k, off in enumerate(OFFSETS)}
OWN = SLOT[0]


def step_kernel(
    acts, cots, inner, first, second, anchor, momentum, first_out, values_out,
    a_buf, c_buf, state, first_buf, go_up, go_down, from_down, from_up,
    drift_buf, drift_pair, pair_sum, z_buf, w_buf, v_send, v_recv, v_out,
    state_sem, cots_own, cots_s, cots_r, acts_own, acts_s, acts_r, up_s, up_r, down_s, down_r,
    pair_s, pair_r, z_s, z_r, wz_s, wz_r, wy_s, wy_r, wc_s, wc_r, v_s, v_r, first_sem, values_sem,
):
    f = lax.axis_index("fsdp")
    r = lax.axis_index("rep")
    y, j = lax.div(f, J), lax.rem(f, J)
    zh, core = lax.div(r, 2), lax.rem(r, 2)
    plane_peer = [lax.rem(j + d, J) for d in range(J)]
    in_plane = [{"fsdp": y * J + plane_peer[d]} for d in range(J)]
    along_y = [{"fsdp": lax.rem(y + t, Y) * J + j} for t in range(Y)]
    along_z = [{"rep": lax.rem(zh + q, Z) * 2 + core} for q in range(Z)]
    sibling = {"rep": zh * 2 + 1 - core}

    def remote(src, dst, send, recv, device):
        return pltpu.make_async_remote_copy(
            src_ref=src, dst_ref=dst, send_sem=send, recv_sem=recv, device_id=device, device_id_type=MESH
        )

    def rows(start, size):
        return pl.ds(pl.multiple_of(start, size), size)

    barrier = pltpu.get_barrier_semaphore()
    for device in in_plane[1:] + along_y[1:] + along_z[1:] + [sibling]:
        pl.semaphore_signal(barrier, inc=1, device_id=device, device_id_type=MESH)

    own_cots = pltpu.make_async_copy(cots, c_buf.at[rows(j * B, B)], cots_own)
    own_cots.start()

    def acts_block(k, target):
        return acts.at[:, rows((lax.rem(y + OFFSETS[k], Y) * J + target) * B, B)]

    own_acts = [
        pltpu.make_async_copy(acts_block(k, j), a_buf.at[rows(j * B, B), pl.ds(k * B, B)], acts_own.at[k])
        for k in range(Y)
    ]
    for copy in own_acts:
        copy.start()
    loads = [
        pltpu.make_async_copy(ref, state.at[i], state_sem.at[i])
        for i, ref in enumerate((inner, first, second, anchor, momentum))
    ]
    for load in loads:
        load.start()
    pl.semaphore_wait(barrier, J - 1 + Y - 1 + Z - 1 + 1)

    for d in range(1, J):
        remote(cots, c_buf.at[rows(j * B, B)], cots_s, cots_r, in_plane[d]).start()
    for k in range(Y):
        for d in range(1, J):
            remote(
                acts_block(k, plane_peer[d]), a_buf.at[rows(j * B, B), pl.ds(k * B, B)],
                acts_s.at[k], acts_r.at[k], in_plane[d],
            ).start()

    others = pl.ds(0, (J - 1) * B)
    all_cots = remote(c_buf.at[others], c_buf.at[others], cots_s, cots_r, in_plane[1])

    def acts_arrivals(k):
        block = a_buf.at[others, pl.ds(k * B, B)]
        return remote(block, block, acts_s.at[k], acts_r.at[k], in_plane[1])

    own_cots.wait()
    all_cots.wait_recv()

    def partial_gradient(k):
        own_acts[k].wait()
        acts_arrivals(k).wait_recv()
        return lax.dot_general(
            a_buf[:, pl.ds(k * B, B)], c_buf[...], (((0,), (0,)), ((), ())), preferred_element_type=F32
        )

    half = C // 2
    halves = (pl.ds(0, half), pl.ds(half, half))
    low, high = halves
    part = partial_gradient(SLOT[4])
    go_up[0, :, low] = part[:, :half]
    go_down[0, :, high] = part[:, half:]

    def up_copy(i):
        cols = low if i == 0 else pl.ds(0, C)
        return remote(go_up.at[i, :, cols], from_down.at[i, :, cols], up_s.at[i], up_r.at[i], along_y[1])

    def down_copy(i):
        cols = high if i == 0 else pl.ds(0, C)
        return remote(go_down.at[i, :, cols], from_up.at[i, :, cols], down_s.at[i], down_r.at[i], along_y[Y - 1])

    ups = [up_copy(i) for i in range(4)]
    downs = [down_copy(i) for i in range(4)]
    ups[0].start()
    downs[0].start()
    for i in range(1, 4):
        part = partial_gradient(SLOT[4 - i])
        ups[i - 1].wait_recv()
        if i == 1:
            go_up[1, :, low] = part[:, :half] + from_down[0, :, low]
            go_up[1, :, high] = part[:, half:]
        else:
            go_up[i] = part + from_down[i - 1]
        ups[i].start()
        part = partial_gradient(SLOT[4 + i])
        downs[i - 1].wait_recv()
        if i == 1:
            go_down[1, :, low] = part[:, :half]
            go_down[1, :, high] = part[:, half:] + from_up[0, :, high]
        else:
            go_down[i] = part + from_up[i - 1]
        downs[i].start()
    drift_buf[...] = partial_gradient(OWN)
    for load in loads:
        load.wait()
    ups[3].wait_recv()
    downs[3].wait_recv()

    H = B // 2
    Q = H // Z
    mine = core * H + zh * Q
    sent = []

    def inner_step(s):
        cols = halves[s]
        gradient = drift_buf[:, cols] + from_down[3, :, cols] + from_up[3, :, cols]
        first_next = decay_first * state[1, :, cols] + (1.0 - decay_first) * gradient
        first_buf[:, cols] = first_next
        second_next = decay_second * state[2, :, cols] + (1.0 - decay_second) * gradient * gradient
        stepped = state[0, :, cols] - inner_rate * first_next / (jnp.sqrt(second_next) + epsilon)
        drift_buf[:, cols] = state[3, :, cols] - stepped
        pairs[s].start()

    pairs = [
        remote(
            drift_buf.at[rows((1 - core) * H, H), halves[s]], drift_pair.at[:, halves[s]],
            pair_s.at[s], pair_r.at[s], sibling,
        )
        for s in range(2)
    ]
    zs = [
        [
            remote(
                pair_sum.at[rows(lax.rem(zh + q, Z) * Q, Q), halves[s]], z_buf.at[q, :, halves[s]],
                z_s.at[s, q], z_r.at[s, q], along_z[q],
            )
            for q in range(1, Z)
        ]
        for s in range(2)
    ]

    def sum_cores(s):
        cols = halves[s]
        pairs[s].wait_recv()
        pair_sum[:, cols] = drift_buf[rows(core * H, H), cols] + drift_pair[:, cols]
        for copy in zs[s]:
            copy.start()

    def wz_copy(s, q):
        here = w_buf.at[rows(OWN * B + mine, Q), halves[s]]
        return remote(here, here, wz_s.at[s, q], wz_r.at[s, q], along_z[q])

    def wz_arrival(s, q):
        there = w_buf.at[rows(OWN * B + core * H + lax.rem(zh + Z - q, Z) * Q, Q), halves[s]]
        return remote(there, there, wz_s.at[s, q], wz_r.at[s, q], along_z[q])

    wzs = [[wz_copy(s, q) for q in range(1, Z)] for s in range(2)]

    def outer_step(s):
        cols = halves[s]
        total = pair_sum[rows(zh * Q, Q), cols]
        for q in range(1, Z):
            zs[s][q - 1].wait_recv()
            total = total + z_buf[q, :, cols]
        average = total / (2 * Z)
        velocity = outer_decay * state[4, rows(mine, Q), cols] + average
        weights = state[3, rows(mine, Q), cols] - outer_rate * (average + outer_decay * velocity)
        w_buf[rows(OWN * B + mine, Q), cols] = weights.astype(BF16)
        for copy in wzs[s]:
            copy.start()

    def w_half(s, t, side):
        return w_buf.at[rows(SLOT[(Y - t) % Y] * B + side * H, H), halves[s]]

    near_first = (4, 3, 5, 2, 6, 1, 7)
    wys = [
        {t: remote(w_half(s, 0, core), w_half(s, t, core), wy_s.at[s, t], wy_r.at[s, t], along_y[t]) for t in near_first}
        for s in range(2)
    ]
    forwards = [
        [remote(w_half(s, t, core), w_half(s, t, core), wc_s.at[s, t], wc_r.at[s, t], sibling) for t in range(Y)]
        for s in range(2)
    ]

    def spread(s):
        for q in range(1, Z):
            wz_arrival(s, q).wait_recv()
        for t in near_first:
            wys[s][t].start()
        forwards[s][0].start()

    def to_sibling(s):
        for t in reversed(near_first):
            wys[s][t].wait_recv()
            forwards[s][t].start()

    def values_of(s, d):
        return jnp.dot(a_buf[rows(plane_peer[d] * B, B), :], w_buf[:, halves[s]], preferred_element_type=F32)

    vs = [
        [remote(v_send.at[s, d], v_recv.at[s, d], v_s.at[s, d], v_r.at[s, d], in_plane[d]) for d in range(1, J)]
        for s in range(2)
    ]

    def send_values(s):
        for t in range(Y):
            there = w_half(s, t, 1 - core)
            remote(there, there, wc_s.at[s, t], wc_r.at[s, t], sibling).wait_recv()
        for d in range(1, J):
            v_send[s, d] = values_of(s, d).astype(BF16)
            vs[s][d - 1].start()

    stores = [
        pltpu.make_async_copy(v_out.at[:, halves[s]], values_out.at[:, halves[s]], values_sem.at[s]) for s in range(2)
    ]

    def sum_values(s):
        total = values_of(s, 0)
        for d in range(1, J):
            vs[s][d - 1].wait_recv()
            total = total + v_recv[s, d].astype(F32)
        v_out[:, halves[s]] = total.astype(BF16)
        stores[s].start()

    inner_step(0)
    inner_step(1)
    store_first = pltpu.make_async_copy(first_buf, first_out, first_sem)
    store_first.start()
    sum_cores(0)
    sum_cores(1)
    outer_step(0)
    outer_step(1)
    spread(0)
    spread(1)
    to_sibling(0)
    send_values(0)
    to_sibling(1)
    send_values(1)
    sum_values(0)
    sum_values(1)

    all_cots.wait_send()
    for k in range(Y):
        acts_arrivals(k).wait_send()
    for copy in ups + downs + pairs:
        copy.wait_send()
    for s in range(2):
        for copy in zs[s] + wzs[s] + list(wys[s].values()) + forwards[s] + vs[s]:
            copy.wait_send()
    store_first.wait()
    for store in stores:
        store.wait()


def on_device(acts, value_cots, inner_weights, first_moment, second_moment, anchor, outer_momentum):
    dma = pltpu.SemaphoreType.DMA
    vmem = pltpu.VMEM
    first_next, values = pl.pallas_call(
        step_kernel,
        name="diloco_step",
        out_shape=(jax.ShapeDtypeStruct((B, C), F32), jax.ShapeDtypeStruct((B, C), BF16)),
        in_specs=[pl.BlockSpec(memory_space=pl.ANY)] * 7,
        out_specs=(pl.BlockSpec(memory_space=pl.ANY), pl.BlockSpec(memory_space=pl.ANY)),
        scratch_shapes=[
            vmem((J * B, Y * B), BF16),
            vmem((J * B, C), BF16),
            vmem((5, B, C), F32),
            vmem((B, C), F32),
            vmem((4, B, C), F32),
            vmem((4, B, C), F32),
            vmem((4, B, C), F32),
            vmem((4, B, C), F32),
            vmem((B, C), F32),
            vmem((B // 2, C), F32),
            vmem((B // 2, C), F32),
            vmem((Z, B // 2 // Z, C), F32),
            vmem((Y * B, C), BF16),
            vmem((2, J, B, C // 2), BF16),
            vmem((2, J, B, C // 2), BF16),
            vmem((B, C), BF16),
            dma((5,)),
            dma(()), dma(()), dma(()),
            dma((Y,)), dma((Y,)), dma((Y,)),
            dma((4,)), dma((4,)), dma((4,)), dma((4,)),
            dma((2,)), dma((2,)),
            dma((2, Z)), dma((2, Z)),
            dma((2, Z)), dma((2, Z)),
            dma((2, Y)), dma((2, Y)),
            dma((2, Y)), dma((2, Y)),
            dma((2, J)), dma((2, J)),
            dma(()), dma((2,)),
        ],
        compiler_params=pltpu.CompilerParams(
            collective_id=0, has_side_effects=True, vmem_limit_bytes=62 * 1024 * 1024
        ),
    )(acts[0], value_cots[0], inner_weights[0], first_moment[0], second_moment[0], anchor, outer_momentum)
    return first_next[None], values[None]


def solution(mesh):
    placed = (
        P("rep", "fsdp", None),
        P("rep", "fsdp", None),
        P("rep", "fsdp", None),
        P("rep", "fsdp", None),
        P("rep", "fsdp", None),
        P("fsdp", None),
        P("fsdp", None),
    )
    return jax.shard_map(
        on_device,
        mesh=mesh,
        in_specs=placed,
        out_specs=(P("rep", "fsdp", None), P("rep", "fsdp", None)),
        check_vma=False,
    )
```

time: 756 us -> 102 us (0.13)
  the two profiles are of different devices: /device:TPU:2 before, /device:TPU:1 now
where the time goes in v2:
time: 102 us
  Pallas kernels  98.4 us (96%)
  local copies, waits for them, and re-layouts  3.24 us (3%)
    pallas_call x1, Pallas kernels, on_device(): pl.pallas_call(step_kernel, name='diloco_step', out_shape=(jax.ShapeDtype...  98.4 us
    unnamed x2, local copies, waits for them, and re-layouts  3.24 us

profile of v2, /device:TPU:1, one launch (start us, length us, event | category | flops | bytes accessed | tf_op | source)
XLA Modules:
  0.0 102.3 jit_solution(5939598842369399211)
XLA Ops:
  0.6 98.4 %diloco_step.1 = (f32[128,512]{1,0:T(8,128)}, bf16[128,512]{1,0:T(8,128)(2,1)}) custom-call(bf16[128,8192]{1,0:T(8,128)(2,1)} %bitcast.7, bf16[128,512]{1,0:T(8,128)(2,1)} %bitcast.12, f32[128,512]{1,0:T(8,128)} %bitcast.8, f32[128,512]{1,0:T(8,128)} %bitcast.9, f32[128,512]{1,0:T(8,128)} %bitcast.10, f32[128,512]{1,0:T(8,128)} %anchor.1, f32[128,512]{1,0:T(8,128)} %momentum.1), custom_call_target="tpu_custom_call" | custom-call | tf_op jit(solution)/shard_map/diloco_step/pallas_call | solution.py:295
  99.0 1.7 %copy.11 = f32[1,128,512]{2,1,0:T(8,128)} copy(f32[1,128,512]{2,1,0:T(8,128)} %bitcast.11) | data formatting | bytes 524288
  100.7 1.6 %copy.12 = bf16[1,128,512]{2,1,0:T(8,128)(2,1)} copy(bf16[1,128,512]{2,1,0:T(8,128)(2,1)} %bitcast.13) | data formatting | bytes 262144

commit v3 on v2

v3 whole, which is shorter than its diff:
```python
import jax
import jax.numpy as jnp
from jax import lax
from jax.experimental import pallas as pl
from jax.experimental.pallas import tpu as pltpu
from jax.sharding import PartitionSpec as P

decay_first = 0.9
decay_second = 0.95
inner_rate = 0.006
epsilon = 1e-08
outer_rate = 0.7
outer_decay = 0.9

MESH = pl.DeviceIdType.MESH
F32 = jnp.float32
BF16 = jnp.bfloat16

Y = 8
J = 8
Z = 4
B = 128
C = 512
OFFSETS = (4, 3, 5, 2, 6, 1, 7, 0)
SLOT = {off: k for k, off in enumerate(OFFSETS)}
OWN = SLOT[0]
CHAIN = 2
SLICES = 4


def step_kernel(
    acts, cots, inner, first, second, anchor, momentum, first_out, values_out,
    a_buf, c_buf, state, first_buf, go_up, go_down, from_down, from_up,
    drift_buf, drift_pair, z_buf, w_buf, v_send, v_recv, v_out,
    state_sem, cots_own, cots_s, cots_r, acts_own, acts_s, acts_r, up_s, up_r, down_s, down_r,
    pair_s, pair_r, z_s, z_r, wy_s, wy_r, wc_s, wc_r, v_s, v_r, first_sem, values_sem,
):
    f = lax.axis_index("fsdp")
    r = lax.axis_index("rep")
    y, j = lax.div(f, J), lax.rem(f, J)
    zh, core = lax.div(r, 2), lax.rem(r, 2)
    plane_peer = [lax.rem(j + d, J) for d in range(J)]
    in_plane = [{"fsdp": y * J + plane_peer[d]} for d in range(J)]
    along_y = [{"fsdp": lax.rem(y + t, Y) * J + j} for t in range(Y)]
    along_z = [{"rep": lax.rem(zh + q, Z) * 2 + core} for q in range(Z)]
    sibling = {"rep": zh * 2 + 1 - core}

    def remote(src, dst, send, recv, device):
        return pltpu.make_async_remote_copy(
            src_ref=src, dst_ref=dst, send_sem=send, recv_sem=recv, device_id=device, device_id_type=MESH
        )

    def rows(start, size):
        return pl.ds(pl.multiple_of(start, size), size)

    barrier = pltpu.get_barrier_semaphore()
    for device in in_plane[1:] + along_y[1:] + along_z[1:] + [sibling]:
        pl.semaphore_signal(barrier, inc=1, device_id=device, device_id_type=MESH)

    own_cots = pltpu.make_async_copy(cots, c_buf.at[rows(j * B, B)], cots_own)
    own_cots.start()

    def acts_block(k, target):
        return acts.at[:, rows((lax.rem(y + OFFSETS[k], Y) * J + target) * B, B)]

    own_acts = [
        pltpu.make_async_copy(acts_block(k, j), a_buf.at[rows(j * B, B), pl.ds(k * B, B)], acts_own.at[k])
        for k in range(Y)
    ]
    for copy in own_acts:
        copy.start()
    loads = [
        pltpu.make_async_copy(ref, state.at[i], state_sem.at[i])
        for i, ref in enumerate((inner, first, second, anchor, momentum))
    ]
    for load in loads:
        load.start()
    pl.semaphore_wait(barrier, J - 1 + Y - 1 + Z - 1 + 1)

    for d in range(1, J):
        remote(cots, c_buf.at[rows(j * B, B)], cots_s, cots_r, in_plane[d]).start()
    for k in range(Y):
        for d in range(1, J):
            remote(
                acts_block(k, plane_peer[d]), a_buf.at[rows(j * B, B), pl.ds(k * B, B)],
                acts_s.at[k], acts_r.at[k], in_plane[d],
            ).start()

    others = pl.ds(0, (J - 1) * B)
    all_cots = remote(c_buf.at[others], c_buf.at[others], cots_s, cots_r, in_plane[1])

    def acts_arrivals(k):
        block = a_buf.at[others, pl.ds(k * B, B)]
        return remote(block, block, acts_s.at[k], acts_r.at[k], in_plane[1])

    own_cots.wait()
    all_cots.wait_recv()

    def partial_gradient(k):
        own_acts[k].wait()
        acts_arrivals(k).wait_recv()
        return lax.dot_general(
            a_buf[:, pl.ds(k * B, B)], c_buf[...], (((0,), (0,)), ((), ())), preferred_element_type=F32
        )

    chain_cols = [pl.ds(s * (C // CHAIN), C // CHAIN) for s in range(CHAIN)]

    def chain(send_buf, recv_buf, send_sem, recv_sem, device):
        return [
            [
                remote(send_buf.at[i, :, cols], recv_buf.at[i, :, cols], send_sem.at[i, s], recv_sem.at[i, s], device)
                for s, cols in enumerate(chain_cols)
            ]
            for i in range(4)
        ]

    ups = chain(go_up, from_down, up_s, up_r, along_y[1])
    downs = chain(go_down, from_up, down_s, down_r, along_y[Y - 1])
    ups_first, downs_first = range(CHAIN // 2), range(CHAIN // 2, CHAIN)

    def add_and_send(i, part, copies, first_slices, send_buf, recv_buf):
        for s in range(CHAIN) if i else first_slices:
            cols = chain_cols[s]
            piece = part[:, s * (C // CHAIN) : (s + 1) * (C // CHAIN)]
            if i > 1 or i == 1 and s in first_slices:
                copies[i - 1][s].wait_recv()
                piece = piece + recv_buf[i - 1, :, cols].astype(F32)
            send_buf[i, :, cols] = piece.astype(BF16)
            copies[i][s].start()

    part = partial_gradient(SLOT[4])
    add_and_send(0, part, ups, ups_first, go_up, from_down)
    add_and_send(0, part, downs, downs_first, go_down, from_up)
    for i in range(1, 4):
        add_and_send(i, partial_gradient(SLOT[4 - i]), ups, ups_first, go_up, from_down)
        add_and_send(i, partial_gradient(SLOT[4 + i]), downs, downs_first, go_down, from_up)
    drift_buf[...] = partial_gradient(OWN)
    for load in loads:
        load.wait()

    H = B // 2
    W = C // SLICES
    slices = [pl.ds(s * W, W) for s in range(SLICES)]

    def inner_step(s):
        cols = slices[s]
        if s * CHAIN % SLICES == 0:
            ups[3][s * CHAIN // SLICES].wait_recv()
            downs[3][s * CHAIN // SLICES].wait_recv()
        gradient = drift_buf[:, cols] + from_down[3, :, cols].astype(F32) + from_up[3, :, cols].astype(F32)
        first_next = decay_first * state[1, :, cols] + (1.0 - decay_first) * gradient
        first_buf[:, cols] = first_next
        second_next = decay_second * state[2, :, cols] + (1.0 - decay_second) * gradient * gradient
        stepped = state[0, :, cols] - inner_rate * first_next / (jnp.sqrt(second_next) + epsilon)
        drift_buf[:, cols] = state[3, :, cols] - stepped
        pairs[s].start()

    pairs = [
        remote(drift_buf.at[rows((1 - core) * H, H), cols], drift_pair.at[:, cols], pair_s.at[s], pair_r.at[s], sibling)
        for s, cols in enumerate(slices)
    ]

    def z_copies(s):
        here = z_buf.at[zh, :, slices[s]]
        return [remote(here, here, z_s.at[s, q], z_r.at[s, q], along_z[q]) for q in range(1, Z)]

    zs = [z_copies(s) for s in range(SLICES)]

    def sum_cores(s):
        cols = slices[s]
        pairs[s].wait_recv()
        z_buf[zh, :, cols] = drift_buf[rows(core * H, H), cols] + drift_pair[:, cols]
        for copy in zs[s]:
            copy.start()

    def w_half(s, t, side):
        return w_buf.at[rows(SLOT[(Y - t) % Y] * B + side * H, H), slices[s]]

    near_first = (4, 3, 5, 2, 6, 1, 7)
    wys = [
        {t: remote(w_half(s, 0, core), w_half(s, t, core), wy_s.at[s, t], wy_r.at[s, t], along_y[t]) for t in near_first}
        for s in range(SLICES)
    ]
    forwards = [
        [remote(w_half(s, t, core), w_half(s, t, core), wc_s.at[s, t], wc_r.at[s, t], sibling) for t in range(Y)]
        for s in range(SLICES)
    ]

    def outer_step(s):
        cols = slices[s]
        for q in range(1, Z):
            there = z_buf.at[lax.rem(zh + Z - q, Z), :, cols]
            remote(there, there, z_s.at[s, q], z_r.at[s, q], along_z[q]).wait_recv()
        total = z_buf[0, :, cols] + z_buf[1, :, cols] + z_buf[2, :, cols] + z_buf[3, :, cols]
        average = total / (2 * Z)
        mine = rows(core * H, H)
        velocity = outer_decay * state[4, mine, cols] + average
        weights = state[3, mine, cols] - outer_rate * (average + outer_decay * velocity)
        w_buf[rows(OWN * B + core * H, H), cols] = weights.astype(BF16)
        for t in near_first:
            wys[s][t].start()
        forwards[s][0].start()

    def to_sibling(s):
        for t in reversed(near_first):
            wys[s][t].wait_recv()
            forwards[s][t].start()

    def values_of(s, d):
        return jnp.dot(a_buf[rows(plane_peer[d] * B, B), :], w_buf[:, slices[s]], preferred_element_type=F32)

    vs = [
        [remote(v_send.at[s, d], v_recv.at[s, d], v_s.at[s, d], v_r.at[s, d], in_plane[d]) for d in range(1, J)]
        for s in range(SLICES)
    ]

    def send_values(s):
        for t in range(Y):
            there = w_half(s, t, 1 - core)
            remote(there, there, wc_s.at[s, t], wc_r.at[s, t], sibling).wait_recv()
        for d in range(1, J):
            v_send[s, d] = values_of(s, d).astype(BF16)
            vs[s][d - 1].start()

    stores = [
        pltpu.make_async_copy(v_out.at[:, cols], values_out.at[:, cols], values_sem.at[s]) for s, cols in enumerate(slices)
    ]

    def sum_values(s):
        total = values_of(s, 0)
        for d in range(1, J):
            vs[s][d - 1].wait_recv()
            total = total + v_recv[s, d].astype(F32)
        v_out[:, slices[s]] = total.astype(BF16)
        stores[s].start()

    for s in range(SLICES):
        inner_step(s)
        if s:
            sum_cores(s - 1)
    sum_cores(SLICES - 1)
    store_first = pltpu.make_async_copy(first_buf, first_out, first_sem)
    store_first.start()
    for s in range(SLICES):
        outer_step(s)
    for s in range(SLICES):
        to_sibling(s)
        send_values(s)
    for s in range(SLICES):
        sum_values(s)

    all_cots.wait_send()
    for k in range(Y):
        acts_arrivals(k).wait_send()
    for copies, first_slices in ((ups, ups_first), (downs, downs_first)):
        for i in range(4):
            for s in range(CHAIN) if i else first_slices:
                copies[i][s].wait_send()
    for s in range(SLICES):
        for copy in [pairs[s]] + zs[s] + list(wys[s].values()) + forwards[s] + vs[s]:
            copy.wait_send()
    store_first.wait()
    for store in stores:
        store.wait()


def on_device(acts, value_cots, inner_weights, first_moment, second_moment, anchor, outer_momentum):
    dma = pltpu.SemaphoreType.DMA
    vmem = pltpu.VMEM
    first_next, values = pl.pallas_call(
        step_kernel,
        name="diloco_step",
        out_shape=(jax.ShapeDtypeStruct((B, C), F32), jax.ShapeDtypeStruct((B, C), BF16)),
        in_specs=[pl.BlockSpec(memory_space=pl.ANY)] * 7,
        out_specs=(pl.BlockSpec(memory_space=pl.ANY), pl.BlockSpec(memory_space=pl.ANY)),
        scratch_shapes=[
            vmem((J * B, Y * B), BF16),
            vmem((J * B, C), BF16),
            vmem((5, B, C), F32),
            vmem((B, C), F32),
            vmem((4, B, C), BF16),
            vmem((4, B, C), BF16),
            vmem((4, B, C), BF16),
            vmem((4, B, C), BF16),
            vmem((B, C), F32),
            vmem((B // 2, C), F32),
            vmem((Z, B // 2, C), F32),
            vmem((Y * B, C), BF16),
            vmem((SLICES, J, B, C // SLICES), BF16),
            vmem((SLICES, J, B, C // SLICES), BF16),
            vmem((B, C), BF16),
            dma((5,)),
            dma(()), dma(()), dma(()),
            dma((Y,)), dma((Y,)), dma((Y,)),
            dma((4, CHAIN)), dma((4, CHAIN)), dma((4, CHAIN)), dma((4, CHAIN)),
            dma((SLICES,)), dma((SLICES,)),
            dma((SLICES, Z)), dma((SLICES, Z)),
            dma((SLICES, Y)), dma((SLICES, Y)),
            dma((SLICES, Y)), dma((SLICES, Y)),
            dma((SLICES, J)), dma((SLICES, J)),
            dma(()), dma((SLICES,)),
        ],
        compiler_params=pltpu.CompilerParams(
            collective_id=0, has_side_effects=True, vmem_limit_bytes=62 * 1024 * 1024
        ),
    )(acts[0], value_cots[0], inner_weights[0], first_moment[0], second_moment[0], anchor, outer_momentum)
    return first_next[None], values[None]


def solution(mesh):
    placed = (
        P("rep", "fsdp", None),
        P("rep", "fsdp", None),
        P("rep", "fsdp", None),
        P("rep", "fsdp", None),
        P("rep", "fsdp", None),
        P("fsdp", None),
        P("fsdp", None),
    )
    return jax.shard_map(
        on_device,
        mesh=mesh,
        in_specs=placed,
        out_specs=(P("rep", "fsdp", None), P("rep", "fsdp", None)),
        check_vma=False,
    )
```

time: 102 us -> 93.6 us (0.918)
  Pallas kernels: 98.4 us -> 89.5 us
    pallas_call x1, Pallas kernels: 98.4 us -> 89.5 us  [on_device(): pl.pallas_call(step_kernel, name='diloco_step', out_shape=(jax.ShapeDtype...]
where the time goes in v3:
time: 93.6 us; the launch traced here: 93.4 us
  Pallas kernels  89.5 us (96%)
  local copies, waits for them, and re-layouts  3.24 us (3%)
    pallas_call x1, Pallas kernels, on_device(): pl.pallas_call(step_kernel, name='diloco_step', out_shape=(jax.ShapeDtype...  89.5 us
    unnamed x2, local copies, waits for them, and re-layouts  3.24 us

profile of v3, /device:TPU:1, one launch (start us, length us, event | category | flops | bytes accessed | tf_op | source)
XLA Modules:
  0.0 93.4 jit_solution(1511881992415512139)
XLA Ops:
  0.6 89.5 %diloco_step.1 = (f32[128,512]{1,0:T(8,128)}, bf16[128,512]{1,0:T(8,128)(2,1)}) custom-call(bf16[128,8192]{1,0:T(8,128)(2,1)} %bitcast.7, bf16[128,512]{1,0:T(8,128)(2,1)} %bitcast.12, f32[128,512]{1,0:T(8,128)} %bitcast.8, f32[128,512]{1,0:T(8,128)} %bitcast.9, f32[128,512]{1,0:T(8,128)} %bitcast.10, f32[128,512]{1,0:T(8,128)} %anchor.1, f32[128,512]{1,0:T(8,128)} %momentum.1), custom_call_target="tpu_custom_call" | custom-call | tf_op jit(solution)/shard_map/diloco_step/pallas_call | solution.py:270
  90.1 1.7 %copy.11 = f32[1,128,512]{2,1,0:T(8,128)} copy(f32[1,128,512]{2,1,0:T(8,128)} %bitcast.11) | data formatting | bytes 524288
  91.8 1.6 %copy.12 = bf16[1,128,512]{2,1,0:T(8,128)(2,1)} copy(bf16[1,128,512]{2,1,0:T(8,128)(2,1)} %bitcast.13) | data formatting | bytes 262144

commit v4 on v3

--- a/solution.py
+++ b/solution.py
@@ -24,6 +24,7 @@
 OFFSETS = (4, 3, 5, 2, 6, 1, 7, 0)
 SLOT = {off: k for k, off in enumerate(OFFSETS)}
 OWN = SLOT[0]
+EARLY = 1
 CHAIN = 2
 SLICES = 4
 
@@ -77,24 +78,55 @@
         load.start()
     pl.semaphore_wait(barrier, J - 1 + Y - 1 + Z - 1 + 1)
 
-    for d in range(1, J):
-        remote(cots, c_buf.at[rows(j * B, B)], cots_s, cots_r, in_plane[d]).start()
-    for k in range(Y):
+    def send_acts(k):
         for d in range(1, J):
             remote(
                 acts_block(k, plane_peer[d]), a_buf.at[rows(j * B, B), pl.ds(k * B, B)],
                 acts_s.at[k], acts_r.at[k], in_plane[d],
             ).start()
 
+    half = C // 2
+    z_piece = j + 1 - 2 * lax.rem(j, 2)
+    z_partner = {"fsdp": y * J + z_piece}
+    along_x = (2, 4, 6)
+
+    def cots_piece(owner, cols):
+        return c_buf.at[rows(owner * B, B), cols]
+
+    every, low_cols, high_cols = pl.ds(0, C), pl.ds(0, half), pl.ds(half, half)
+    own_piece = cots_piece(j, every)
+    remote(cots, own_piece, cots_s.at[0], cots_r.at[0], z_partner).start()
+    for d in along_x:
+        remote(cots, own_piece, cots_s.at[1], cots_r.at[1], in_plane[d]).start()
+    for k in range(EARLY):
+        send_acts(k)
+    three = pl.ds(0, len(along_x) * B)
+    cots_groups = [
+        remote(c_buf.at[r, c], c_buf.at[r, c], cots_s.at[i], cots_r.at[i], z_partner)
+        for i, (r, c) in enumerate(
+            ((pl.ds(0, B), every), (three, every), (three, low_cols), (three, high_cols))
+        )
+    ]
+    cots_groups[0].wait_recv()
+    for d in along_x:
+        piece = cots_piece(z_piece, high_cols)
+        remote(piece, piece, cots_s.at[3], cots_r.at[3], in_plane[d]).start()
+    cots_groups[1].wait_recv()
+    for d in along_x:
+        piece = cots_piece(plane_peer[d], low_cols)
+        remote(piece, piece, cots_s.at[2], cots_r.at[2], z_partner).start()
+    for k in range(EARLY, Y):
+        send_acts(k)
+
     others = pl.ds(0, (J - 1) * B)
-    all_cots = remote(c_buf.at[others], c_buf.at[others], cots_s, cots_r, in_plane[1])
 
     def acts_arrivals(k):
         block = a_buf.at[others, pl.ds(k * B, B)]
         return remote(block, block, acts_s.at[k], acts_r.at[k], in_plane[1])
 
     own_cots.wait()
-    all_cots.wait_recv()
+    cots_groups[2].wait_recv()
+    cots_groups[3].wait_recv()
 
     def partial_gradient(k):
         own_acts[k].wait()
@@ -169,7 +201,7 @@
     def sum_cores(s):
         cols = slices[s]
         pairs[s].wait_recv()
-        z_buf[zh, :, cols] = drift_buf[rows(core * H, H), cols] + drift_pair[:, cols]
+        z_buf[zh, :, cols] = (drift_buf[rows(core * H, H), cols] + drift_pair[:, cols]).astype(BF16)
         for copy in zs[s]:
             copy.start()
 
@@ -191,7 +223,8 @@
         for q in range(1, Z):
             there = z_buf.at[lax.rem(zh + Z - q, Z), :, cols]
             remote(there, there, z_s.at[s, q], z_r.at[s, q], along_z[q]).wait_recv()
-        total = z_buf[0, :, cols] + z_buf[1, :, cols] + z_buf[2, :, cols] + z_buf[3, :, cols]
+        sums = [z_buf[q, :, cols].astype(F32) for q in range(Z)]
+        total = sums[0] + sums[1] + sums[2] + sums[3]
         average = total / (2 * Z)
         mine = rows(core * H, H)
         velocity = outer_decay * state[4, mine, cols] + average
@@ -249,7 +282,8 @@
     for s in range(SLICES):
         sum_values(s)
 
-    all_cots.wait_send()
+    for copies in cots_groups:
+        copies.wait_send()
     for k in range(Y):
         acts_arrivals(k).wait_send()
     for copies, first_slices in ((ups, ups_first), (downs, downs_first)):
@@ -284,13 +318,13 @@
             vmem((4, B, C), BF16),
             vmem((B, C), F32),
             vmem((B // 2, C), F32),
-            vmem((Z, B // 2, C), F32),
+            vmem((Z, B // 2, C), BF16),
             vmem((Y * B, C), BF16),
             vmem((SLICES, J, B, C // SLICES), BF16),
             vmem((SLICES, J, B, C // SLICES), BF16),
             vmem((B, C), BF16),
             dma((5,)),
-            dma(()), dma(()), dma(()),
+            dma(()), dma((4,)), dma((4,)),
             dma((Y,)), dma((Y,)), dma((Y,)),
             dma((4, CHAIN)), dma((4, CHAIN)), dma((4, CHAIN)), dma((4, CHAIN)),
             dma((SLICES,)), dma((SLICES,)),

time: 93.6 us -> 87.5 us (0.935)
  Pallas kernels: 89.5 us -> 83.5 us
    pallas_call x1, Pallas kernels: 89.5 us -> 83.5 us  [on_device(): pl.pallas_call(step_kernel, name='diloco_step', out_shape=(jax.ShapeDtype...]
where the time goes in v4:
time: 87.5 us; the launch traced here: 87.3 us
  Pallas kernels  83.5 us (95%)
  local copies, waits for them, and re-layouts  3.24 us (4%)
    pallas_call x1, Pallas kernels, on_device(): pl.pallas_call(step_kernel, name='diloco_step', out_shape=(jax.ShapeDtype...  83.5 us
    unnamed x2, local copies, waits for them, and re-layouts  3.24 us

profile of v4, /device:TPU:1, one launch (start us, length us, event | category | flops | bytes accessed | tf_op | source)
XLA Modules:
  0.0 87.3 jit_solution(18087757529488736849)
XLA Ops:
  0.6 83.5 %diloco_step.1 = (f32[128,512]{1,0:T(8,128)}, bf16[128,512]{1,0:T(8,128)(2,1)}) custom-call(bf16[128,8192]{1,0:T(8,128)(2,1)} %bitcast.7, bf16[128,512]{1,0:T(8,128)(2,1)} %bitcast.12, f32[128,512]{1,0:T(8,128)} %bitcast.8, f32[128,512]{1,0:T(8,128)} %bitcast.9, f32[128,512]{1,0:T(8,128)} %bitcast.10, f32[128,512]{1,0:T(8,128)} %anchor.1, f32[128,512]{1,0:T(8,128)} %momentum.1), custom_call_target="tpu_custom_call" | custom-call | tf_op jit(solution)/shard_map/diloco_step/pallas_call | solution.py:304
  84.1 1.7 %copy.11 = f32[1,128,512]{2,1,0:T(8,128)} copy(f32[1,128,512]{2,1,0:T(8,128)} %bitcast.11) | data formatting | bytes 524288
  85.8 1.6 %copy.12 = bf16[1,128,512]{2,1,0:T(8,128)(2,1)} copy(bf16[1,128,512]{2,1,0:T(8,128)(2,1)} %bitcast.13) | data formatting | bytes 262144

commit v5 on v4

--- a/solution.py
+++ b/solution.py
@@ -32,7 +32,7 @@
 def step_kernel(
     acts, cots, inner, first, second, anchor, momentum, first_out, values_out,
     a_buf, c_buf, state, first_buf, go_up, go_down, from_down, from_up,
-    drift_buf, drift_pair, z_buf, w_buf, v_send, v_recv, v_out,
+    stepped_buf, stepped_pair, z_buf, w_buf, v_send, v_recv, v_out,
     state_sem, cots_own, cots_s, cots_r, acts_own, acts_s, acts_r, up_s, up_r, down_s, down_r,
     pair_s, pair_r, z_s, z_r, wy_s, wy_r, wc_s, wc_r, v_s, v_r, first_sem, values_sem,
 ):
@@ -166,7 +166,9 @@
     for i in range(1, 4):
         add_and_send(i, partial_gradient(SLOT[4 - i]), ups, ups_first, go_up, from_down)
         add_and_send(i, partial_gradient(SLOT[4 + i]), downs, downs_first, go_down, from_up)
-    drift_buf[...] = partial_gradient(OWN)
+    own_acts[OWN].wait()
+    acts_arrivals(OWN).wait_recv()
+    own_block = a_buf[:, pl.ds(OWN * B, B)].T
     for load in loads:
         load.wait()
 
@@ -179,16 +181,17 @@
         if s * CHAIN % SLICES == 0:
             ups[3][s * CHAIN // SLICES].wait_recv()
             downs[3][s * CHAIN // SLICES].wait_recv()
-        gradient = drift_buf[:, cols] + from_down[3, :, cols].astype(F32) + from_up[3, :, cols].astype(F32)
+        part = jnp.dot(own_block, c_buf[:, cols], preferred_element_type=F32)
+        gradient = part + from_down[3, :, cols].astype(F32) + from_up[3, :, cols].astype(F32)
         first_next = decay_first * state[1, :, cols] + (1.0 - decay_first) * gradient
         first_buf[:, cols] = first_next
         second_next = decay_second * state[2, :, cols] + (1.0 - decay_second) * gradient * gradient
         stepped = state[0, :, cols] - inner_rate * first_next / (jnp.sqrt(second_next) + epsilon)
-        drift_buf[:, cols] = state[3, :, cols] - stepped
+        stepped_buf[:, cols] = stepped
         pairs[s].start()
 
     pairs = [
-        remote(drift_buf.at[rows((1 - core) * H, H), cols], drift_pair.at[:, cols], pair_s.at[s], pair_r.at[s], sibling)
+        remote(stepped_buf.at[rows((1 - core) * H, H), cols], stepped_pair.at[:, cols], pair_s.at[s], pair_r.at[s], sibling)
         for s, cols in enumerate(slices)
     ]
 
@@ -201,7 +204,7 @@
     def sum_cores(s):
         cols = slices[s]
         pairs[s].wait_recv()
-        z_buf[zh, :, cols] = (drift_buf[rows(core * H, H), cols] + drift_pair[:, cols]).astype(BF16)
+        z_buf[zh, :, cols] = (stepped_buf[rows(core * H, H), cols] + stepped_pair[:, cols]).astype(BF16)
         for copy in zs[s]:
             copy.start()
 
@@ -225,8 +228,8 @@
             remote(there, there, z_s.at[s, q], z_r.at[s, q], along_z[q]).wait_recv()
         sums = [z_buf[q, :, cols].astype(F32) for q in range(Z)]
         total = sums[0] + sums[1] + sums[2] + sums[3]
-        average = total / (2 * Z)
         mine = rows(core * H, H)
+        average = state[3, mine, cols] - total / (2 * Z)
         velocity = outer_decay * state[4, mine, cols] + average
         weights = state[3, mine, cols] - outer_rate * (average + outer_decay * velocity)
         w_buf[rows(OWN * B + core * H, H), cols] = weights.astype(BF16)
@@ -269,9 +272,7 @@
 
     for s in range(SLICES):
         inner_step(s)
-        if s:
-            sum_cores(s - 1)
-    sum_cores(SLICES - 1)
+        sum_cores(s)
     store_first = pltpu.make_async_copy(first_buf, first_out, first_sem)
     store_first.start()
     for s in range(SLICES):

time: 87.5 us -> 87 us (level)
  no operation moved by 1% of the time
where the time goes in v5:
time: 87 us; the launch traced here: 86.8 us
  Pallas kernels  83 us (95%)
  local copies, waits for them, and re-layouts  3.24 us (4%)
    pallas_call x1, Pallas kernels, on_device(): pl.pallas_call(step_kernel, name='diloco_step', out_shape=(jax.ShapeDtype...  83 us
    unnamed x2, local copies, waits for them, and re-layouts  3.24 us

profile of v5, /device:TPU:1, one launch (start us, length us, event | category | flops | bytes accessed | tf_op | source)
XLA Modules:
  0.0 86.8 jit_solution(17759600732127965544)
XLA Ops:
  0.6 83.0 %diloco_step.1 = (f32[128,512]{1,0:T(8,128)}, bf16[128,512]{1,0:T(8,128)(2,1)}) custom-call(bf16[128,8192]{1,0:T(8,128)(2,1)} %bitcast.7, bf16[128,512]{1,0:T(8,128)(2,1)} %bitcast.12, f32[128,512]{1,0:T(8,128)} %bitcast.8, f32[128,512]{1,0:T(8,128)} %bitcast.9, f32[128,512]{1,0:T(8,128)} %bitcast.10, f32[128,512]{1,0:T(8,128)} %anchor.1, f32[128,512]{1,0:T(8,128)} %momentum.1), custom_call_target="tpu_custom_call" | custom-call | tf_op jit(solution)/shard_map/diloco_step/pallas_call | solution.py:305
  83.6 1.7 %copy.11 = f32[1,128,512]{2,1,0:T(8,128)} copy(f32[1,128,512]{2,1,0:T(8,128)} %bitcast.11) | data formatting | bytes 524288
  85.3 1.6 %copy.12 = bf16[1,128,512]{2,1,0:T(8,128)(2,1)} copy(bf16[1,128,512]{2,1,0:T(8,128)(2,1)} %bitcast.13) | data formatting | bytes 262144

commit v6 on v5

--- a/solution.py
+++ b/solution.py
@@ -209,7 +209,12 @@
             copy.start()
 
     def w_half(s, t, side):
-        return w_buf.at[rows(SLOT[(Y - t) % Y] * B + side * H, H), slices[s]]
+        return w_buf.at[SLOT[(Y - t) % Y], rows(side * H, H), slices[s]]
+
+    def w_group(s, t, side):
+        if t in (0, 4):
+            return w_half(s, t, side)
+        return w_buf.at[pl.ds(SLOT[t], 2), rows(side * H, H), slices[s]]
 
     near_first = (4, 3, 5, 2, 6, 1, 7)
     wys = [
@@ -217,7 +222,7 @@
         for s in range(SLICES)
     ]
     forwards = [
-        [remote(w_half(s, t, core), w_half(s, t, core), wc_s.at[s, t], wc_r.at[s, t], sibling) for t in range(Y)]
+        [remote(w_group(s, t, core), w_group(s, t, core), wc_s.at[s, t], wc_r.at[s, t], sibling) for t in range(5)]
         for s in range(SLICES)
     ]
 
@@ -232,18 +237,20 @@
         average = state[3, mine, cols] - total / (2 * Z)
         velocity = outer_decay * state[4, mine, cols] + average
         weights = state[3, mine, cols] - outer_rate * (average + outer_decay * velocity)
-        w_buf[rows(OWN * B + core * H, H), cols] = weights.astype(BF16)
+        w_buf[OWN, rows(core * H, H), cols] = weights.astype(BF16)
         for t in near_first:
             wys[s][t].start()
         forwards[s][0].start()
 
     def to_sibling(s):
-        for t in reversed(near_first):
+        for t in range(1, 5):
             wys[s][t].wait_recv()
+            if t < 4:
+                wys[s][Y - t].wait_recv()
             forwards[s][t].start()
 
     def values_of(s, d):
-        return jnp.dot(a_buf[rows(plane_peer[d] * B, B), :], w_buf[:, slices[s]], preferred_element_type=F32)
+        return jnp.dot(a_buf[rows(plane_peer[d] * B, B), :], w_buf[:, :, slices[s]].reshape(Y * B, W), preferred_element_type=F32)
 
     vs = [
         [remote(v_send.at[s, d], v_recv.at[s, d], v_s.at[s, d], v_r.at[s, d], in_plane[d]) for d in range(1, J)]
@@ -251,10 +258,10 @@
     ]
 
     def send_values(s):
-        for t in range(Y):
-            there = w_half(s, t, 1 - core)
+        for t in range(5):
+            there = w_group(s, t, 1 - core)
             remote(there, there, wc_s.at[s, t], wc_r.at[s, t], sibling).wait_recv()
-        for d in range(1, J):
+        for d in (4, 3, 5, 2, 6, 1, 7):
             v_send[s, d] = values_of(s, d).astype(BF16)
             vs[s][d - 1].start()
 
@@ -320,7 +327,7 @@
             vmem((B, C), F32),
             vmem((B // 2, C), F32),
             vmem((Z, B // 2, C), BF16),
-            vmem((Y * B, C), BF16),
+            vmem((Y, B, C), BF16),
             vmem((SLICES, J, B, C // SLICES), BF16),
             vmem((SLICES, J, B, C // SLICES), BF16),
             vmem((B, C), BF16),

time: 87 us -> 87.1 us (level)
  no operation moved by 1% of the time
where the time goes in v6:
time: 87.1 us; the launch traced here: 86.9 us
  Pallas kernels  83 us (95%)
  local copies, waits for them, and re-layouts  3.24 us (4%)
    pallas_call x1, Pallas kernels, on_device(): pl.pallas_call(step_kernel, name='diloco_step', out_shape=(jax.ShapeDtype...  83 us
    unnamed x2, local copies, waits for them, and re-layouts  3.24 us

profile of v6, /device:TPU:1, one launch (start us, length us, event | category | flops | bytes accessed | tf_op | source)
XLA Modules:
  0.0 86.9 jit_solution(1536262312048001171)
XLA Ops:
  0.6 83.0 %diloco_step.1 = (f32[128,512]{1,0:T(8,128)}, bf16[128,512]{1,0:T(8,128)(2,1)}) custom-call(bf16[128,8192]{1,0:T(8,128)(2,1)} %bitcast.7, bf16[128,512]{1,0:T(8,128)(2,1)} %bitcast.12, f32[128,512]{1,0:T(8,128)} %bitcast.8, f32[128,512]{1,0:T(8,128)} %bitcast.9, f32[128,512]{1,0:T(8,128)} %bitcast.10, f32[128,512]{1,0:T(8,128)} %anchor.1, f32[128,512]{1,0:T(8,128)} %momentum.1), custom_call_target="tpu_custom_call" | custom-call | tf_op jit(solution)/shard_map/diloco_step/pallas_call | solution.py:312
  83.6 1.7 %copy.11 = f32[1,128,512]{2,1,0:T(8,128)} copy(f32[1,128,512]{2,1,0:T(8,128)} %bitcast.11) | data formatting | bytes 524288
  85.3 1.6 %copy.12 = bf16[1,128,512]{2,1,0:T(8,128)(2,1)} copy(bf16[1,128,512]{2,1,0:T(8,128)(2,1)} %bitcast.13) | data formatting | bytes 262144

commit v7 on v6

--- a/solution.py
+++ b/solution.py
@@ -261,7 +261,7 @@
         for t in range(5):
             there = w_group(s, t, 1 - core)
             remote(there, there, wc_s.at[s, t], wc_r.at[s, t], sibling).wait_recv()
-        for d in (4, 3, 5, 2, 6, 1, 7):
+        for d in range(1, J):
             v_send[s, d] = values_of(s, d).astype(BF16)
             vs[s][d - 1].start()
 

time: 87.1 us -> 87 us (level)
  no operation moved by 1% of the time
where the time goes in v7:
time: 87 us; the launch traced here: 86.9 us
  Pallas kernels  83 us (95%)
  local copies, waits for them, and re-layouts  3.24 us (4%)
    pallas_call x1, Pallas kernels, on_device(): pl.pallas_call(step_kernel, name='diloco_step', out_shape=(jax.ShapeDtype...  83 us
    unnamed x2, local copies, waits for them, and re-layouts  3.24 us

profile of v7, /device:TPU:1, one launch (start us, length us, event | category | flops | bytes accessed | tf_op | source)
XLA Modules:
  0.0 86.9 jit_solution(8173416461058448672)
XLA Ops:
  0.6 83.0 %diloco_step.1 = (f32[128,512]{1,0:T(8,128)}, bf16[128,512]{1,0:T(8,128)(2,1)}) custom-call(bf16[128,8192]{1,0:T(8,128)(2,1)} %bitcast.7, bf16[128,512]{1,0:T(8,128)(2,1)} %bitcast.12, f32[128,512]{1,0:T(8,128)} %bitcast.8, f32[128,512]{1,0:T(8,128)} %bitcast.9, f32[128,512]{1,0:T(8,128)} %bitcast.10, f32[128,512]{1,0:T(8,128)} %anchor.1, f32[128,512]{1,0:T(8,128)} %momentum.1), custom_call_target="tpu_custom_call" | custom-call | tf_op jit(solution)/shard_map/diloco_step/pallas_call | solution.py:312
  83.6 1.7 %copy.11 = f32[1,128,512]{2,1,0:T(8,128)} copy(f32[1,128,512]{2,1,0:T(8,128)} %bitcast.11) | data formatting | bytes 524288
  85.3 1.6 %copy.12 = bf16[1,128,512]{2,1,0:T(8,128)(2,1)} copy(bf16[1,128,512]{2,1,0:T(8,128)(2,1)} %bitcast.13) | data formatting | bytes 262144
